TPU v7x, 256 devices: a whole 4x4x8 slice. The times are simulated.
256 devices in a mesh: replica: 32 (over x_lo, z, core), tensor: 8 (over y, x_hi).
Axes of the slice: x: 4 (x_hi: 2, x_lo: 2; x = x_hi * 2 + x_lo), y: 4, z: 8, core: 2. Of those that a mesh axis runs over, the one named last changes fastest.
Arguments:
- inputs: bfloat16 [2, 16384, 2048], P(None, 'replica', 'tensor'), may hold values from -6 to 6
- out_grads: bfloat16 [2, 16384, 2048], P(None, 'replica', 'tensor'), may hold values from -6 to 6
- gate_weight: bfloat16 [32, 2048, 2816], P('replica', None, 'tensor'), may hold values from -0.125 to 0.125
- up_weight: bfloat16 [32, 2048, 2816], P('replica', None, 'tensor'), may hold values from -0.125 to 0.125
- down_weight: bfloat16 [32, 2816, 2048], P('replica', 'tensor'), may hold values from -0.109375 to 0.109375
- rates: float32 [32], P('replica'), may hold values from 16 to 64
- partner_bits: int32 [4], replicated, may hold values from 0 to 3, each once
Outputs:
- new_gate: bfloat16 [32, 2048, 2816], P('replica', None, 'tensor')
- new_up: bfloat16 [32, 2048, 2816], P('replica', None, 'tensor')
- new_down: bfloat16 [32, 2816, 2048], P('replica', 'tensor')
- activations: bfloat16 [2, 16384, 2048], P(None, 'replica', 'tensor')
Inputs may be any that keep to these rules, and one draw needn't show every extreme that they name: partner_bits holds each of the bit numbers 0, 1, 2, 3 exactly once; step s uses entry s.
All inputs are finite; a program needn't handle non-finite values.
Results may differ from a plain program's by a relative error of at most 0.024.
Values may be sent and summed in bfloat16 or wider, within the bound.
No kernel may reach another device: no remote copies, remote signals or barrier semaphores. Data moves between devices by JAX's collectives and lax.ppermute only.
A program may use at most 128 MiB of HBM per device.

v0:
```python
from functools import partial
import jax
import jax.numpy as jnp
from jax import lax
from jax.sharding import PartitionSpec as P


def shortened(value):

    def short(part):
        return part.astype(jnp.bfloat16) if part.dtype == jnp.float32 else part

    return jax.tree.map(short, value)


def partner(value, axis, distance):
    mask = 2**distance
    pairs = [(source, source ^ mask) for source in range(lax.axis_size(axis))]
    return lax.ppermute(value, axis, pairs)


def local_pass(weights, inputs, grads_out):
    gate_w, up_w, down_w = weights
    gate = jnp.dot(inputs, gate_w, preferred_element_type=jnp.float32)
    up = jnp.dot(inputs, up_w, preferred_element_type=jnp.float32)
    sigma = jax.nn.sigmoid(gate)
    active = gate * sigma
    hidden = (active * up).astype(jnp.bfloat16)
    mixed = jnp.dot(hidden, down_w, preferred_element_type=jnp.float32)
    back = lax.dot_general(
        grads_out, down_w, (((1,), (1,)), ((), ())), preferred_element_type=jnp.float32
    )
    d_gate = (back * up * sigma * (1.0 + gate * (1.0 - sigma))).astype(jnp.bfloat16)
    d_up = (back * active).astype(jnp.bfloat16)
    grad_down = lax.dot_general(
        hidden, grads_out, (((0,), (0,)), ((), ())), preferred_element_type=jnp.float32
    )
    grad_gate = lax.dot_general(
        inputs, d_gate, (((0,), (0,)), ((), ())), preferred_element_type=jnp.float32
    )
    grad_up = lax.dot_general(
        inputs, d_up, (((0,), (0,)), ((), ())), preferred_element_type=jnp.float32
    )
    return (mixed, (grad_gate, grad_up, grad_down))


def squares_of(grads):
    return sum((jnp.sum(g * g) for g in grads))


def apply_update(weights, grads, squares, rate):
    scale = rate / jnp.sqrt(squares + 1e-06)
    return tuple(
        ((w.astype(jnp.float32) - scale * g).astype(jnp.bfloat16) for w, g in zip(weights, grads))
    )


def average(first, second):
    return tuple(
        (
            ((a.astype(jnp.float32) + b.astype(jnp.float32)) * 0.5).astype(jnp.bfloat16)
            for a, b in zip(first, second)
        )
    )


def total_norms(values):
    return lax.psum((values[0],), "tensor")


def mixing_bit(bit_number, values):
    return jax.tree.map(
        lambda piece: jax.tree.map(
            lambda part, own: part.astype(own.dtype),
            partner(shortened(piece), "replica", bit_number),
            piece,
        ),
        values,
    )


def partner_values(values, bit, handler):
    branches = [partial(handler, number) for number in range(4)]
    return lax.switch(bit, branches, values)


def local(inputs, out_grads, gate_weight, up_weight, down_weight, rates, partner_bits):
    weights = (gate_weight[0], up_weight[0], down_weight[0])
    results = []
    for step in range(inputs.shape[0]):
        whole_x, whole_dy = (
            lax.all_gather(inputs[step], "tensor", axis=1, tiled=True),
            lax.all_gather(out_grads[step], "tensor", axis=1, tiled=True),
        )
        bit = partner_bits[step]
        mixed, grads = local_pass(weights, whole_x, whole_dy)
        squares = total_norms((squares_of(grads),))[0]
        fresh = apply_update(weights, grads, squares, rates[0])
        other = partner_values(fresh, bit, mixing_bit)
        weights = average(fresh, other)
        summed = lax.psum_scatter(
            mixed.astype(jnp.bfloat16), "tensor", scatter_dimension=1, tiled=True
        )
        results.append(summed)
    return (weights[0][None], weights[1][None], weights[2][None], jnp.stack(results))


def solution(mesh):
    return jax.shard_map(
        local,
        mesh=mesh,
        in_specs=(
            P(None, "replica", "tensor"),
            P(None, "replica", "tensor"),
            P("replica", None, "tensor"),
            P("replica", None, "tensor"),
            P("replica", "tensor", None),
            P("replica"),
            P(),
        ),
        out_specs=(
            P("replica", None, "tensor"),
            P("replica", None, "tensor"),
            P("replica", "tensor", None),
            P(None, "replica", "tensor"),
        ),
        check_vma=False,
    )
```

profile of v0, /device:TPU:32, one launch (start us, length us, event | category | flops | bytes accessed | tf_op | source)
XLA Modules:
  0.0 427.8 jit_solution(12777738690879736687)
XLA Ops:
  7.2 0.0 copy-start.14
  7.2 0.0 all-gather.11.cloned.1.call-start
  7.2 2.0 fusion.73
  9.2 0.0 all-gather.11.cloned.1.call-update
  9.2 0.0 all-gather.9.cloned.1.call-start
  9.3 1.9 fusion.72
  11.1 0.0 all-gather.9.cloned.1.call-update
  11.2 0.0 all-gather.15.cloned.1.call-start
  11.2 0.7 all-gather.15.cloned.1.call-update
  11.9 0.0 all-gather.13.cloned.1.call-start
  11.9 0.5 all-gather.13.cloned.1.call-update
  12.5 0.0 reduce-scatter.3.cloned.1.call-start
  13.2 0.6 fusion.74
  13.8 59.1 %all-gather.11.cloned.1.call-done = bf16[1,512,2048]{2,1,0:T(8,128)(2,1)} async-done(((bf16[1,512,256]{2,1,0:T(8,128)(2,1)}), bf16[1,512,2048]{2,1,0:T(8,128)(2,1)}) %all-gather.11.cloned.1.call-update) | async-done | bytes 2097168 | tf_op jit(solution)/shard_map/all_gather | solution.py:92
  72.8 2.7 fusion.32
  75.6 1.9 multiply_convert_fusion.3
  77.5 2.7 convolution_convert_fusion.1
  80.1 0.0 reduce-scatter.3.cloned.1.call-update
  80.2 0.0 reduce-scatter.5.cloned.1.call-start
  80.2 52.8 %all-gather.9.cloned.1.call-done = bf16[1,512,2048]{2,1,0:T(8,128)(2,1)} async-done(((bf16[1,512,256]{2,1,0:T(8,128)(2,1)}), bf16[1,512,2048]{2,1,0:T(8,128)(2,1)}) %all-gather.9.cloned.1.call-update) | async-done | bytes 2097168 | tf_op jit(solution)/shard_map/all_gather | solution.py:93
  133.0 2.7 fusion.38
  135.7 3.2 multiply_reduce_fusion.4
  138.9 3.3 multiply_reduce_fusion.5
  143.5 3.2 multiply_reduce_fusion.3
  147.9 20.4 %psum.14 = f32[]{:T(128)} all-reduce(f32[]{:T(128)S(6)} %add.59), channel_id=1, replica_groups=mesh['replica'=32,'tensor'=8] {'tensor'}, use_global_device_ids=true, to_apply=%region_3.0 | all-reduce | flops 1 | bytes 8 | tf_op jit(solution)/shard_map/psum | solution.py:68
  169.0 2.0 subtract_convert_fusion.1
  171.1 0.2 copy-done.8
  171.3 0.4 copy-done.13
  171.7 0.5 fusion.14
  172.2 1.9 copy-done.9
  174.1 0.4 copy-done.15
  174.5 0.5 fusion.15
  175.0 90.9 %conditional.8 = (bf16[2048,352]{0,1:T(8,128)(2,1)}, bf16[352,2048]{1,0:T(8,128)(2,1)}, bf16[2048,352]{0,1:T(8,128)(2,1)}) conditional(s32[]{:T(128)} %bitcast.7, (bf16[2048,352]{0,1:T(8,128)(2,1)S(1)}, bf16[2048,352]{0,1:T(8,128)(2,1)S(1)}, bf16[352,2048]{1,0:T(8,128)(2,1)S(1)}) %tuple.108, ...), branch_computations={%region_4.0_spmd, %region_5.0_spmd, %region_6.0_spmd, %region_7.0_... | conditional | bytes 17301648
  175.0 0.6 collective-permute-start.3
  175.6 1.5 collective-permute-start.4
  177.2 0.5 collective-permute-start.5
  177.6 32.1 %collective-permute-done.3 = bf16[2048,352]{0,1:T(8,128)(2,1)} collective-permute-done((bf16[2048,352]{0,1:T(8,128)(2,1)S(1)}, bf16[2048,352]{0,1:T(8,128)(2,1)}, u32[]{:S(2)}, u32[]{:S(2)}) %collective-permute-start.3) | collective-permute-done | bytes 1441824 | tf_op jit(solution)/shard_map/cond/branch_1_fun/ppermute | solution.py:19
  209.7 30.9 %collective-permute-done.4 = bf16[2048,352]{0,1:T(8,128)(2,1)} collective-permute-done((bf16[2048,352]{0,1:T(8,128)(2,1)S(1)}, bf16[2048,352]{0,1:T(8,128)(2,1)}, u32[]{:S(2)}, u32[]{:S(2)}) %collective-permute-start.4) | collective-permute-done | bytes 1441824 | tf_op jit(solution)/shard_map/cond/branch_1_fun/ppermute | solution.py:19
  240.6 25.3 %collective-permute-done.5 = bf16[352,2048]{1,0:T(8,128)(2,1)} collective-permute-done((bf16[352,2048]{1,0:T(8,128)(2,1)S(1)}, bf16[352,2048]{1,0:T(8,128)(2,1)}, u32[]{:S(2)}, u32[]{:S(2)}) %collective-permute-start.5) | collective-permute-done | bytes 1441824 | tf_op jit(solution)/shard_map/cond/branch_1_fun/ppermute | solution.py:19
  265.9 3.1 fusion.53
  269.1 3.5 multiply_convert_fusion
  272.6 4.0 convolution_convert_fusion
  276.6 0.0 reduce-scatter.5.cloned.1.call-update
  276.6 0.0 all-gather.13.cloned.1.call-done
  276.6 3.2 fusion.47
  279.9 3.1 multiply_reduce_fusion.1
  283.0 3.3 multiply_reduce_fusion.2
  287.5 3.2 multiply_reduce_fusion
  292.0 22.9 %psum.15 = f32[]{:T(128)} all-reduce(f32[]{:T(128)S(6)} %add.67), channel_id=1, replica_groups=mesh['replica'=32,'tensor'=8] {'tensor'}, use_global_device_ids=true, to_apply=%region_11.0 | all-reduce | flops 1 | bytes 8 | tf_op jit(solution)/shard_map/psum | solution.py:68
  315.5 2.6 subtract_convert_fusion
  318.2 0.9 copy-done.10
  319.0 4.4 %fusion.12 = (bf16[2048,352]{0,1:T(8,128)(2,1)S(1)}, bf16[2048,352]{0,1:T(8,128)(2,1)S(1)}) fusion(f32[352,2048]{1,0:T(8,128)S(1)} %copy-done.10, f32[]{:T(128)S(6)} %div.15, bf16[2048,352]{0,1:T(8,128)(2,1)} %get-tuple-element.159, bf16[2048,352]{0,1:T(8,128)(2,1)S(1)} %copy-done.5, f32[352,2048]{1,0:T(8,128)} %get-tuple-element.181, ...), kind=kLoop, calls=%fused_computation.21 | loop fusion | flops 12976128 | bytes 14417924 | tf_op jit(solution)/shard_map/convert_element_type | solution.py:54
  323.5 7.6 %conditional.9 = (bf16[2048,352]{0,1:T(8,128)(2,1)}, bf16[2048,352]{0,1:T(8,128)(2,1)}, bf16[352,2048]{1,0:T(8,128)(2,1)}) conditional(s32[]{:T(128)} %bitcast.15, (bf16[2048,352]{0,1:T(8,128)(2,1)S(1)}, bf16[2048,352]{0,1:T(8,128)(2,1)S(1)}, bf16[352,2048]{1,0:T(8,128)(2,1)S(1)}) %tuple.109, ...), branch_computations={%region_12.0_spmd, %region_13.0_spmd, %region_14.0_spmd, %region_1... | conditional | bytes 17301648
  323.5 0.1 collective-permute-start.12
  323.6 0.5 collective-permute-start.13
  324.1 0.1 collective-permute-start.14
  324.2 2.7 collective-permute-done.12
  326.9 2.1 collective-permute-done.13
  329.0 2.1 collective-permute-done.14
  331.0 3.1 fusion.40
  334.1 3.0 fusion.42
  337.1 3.0 fusion.41
  340.1 79.1 %reduce-scatter.5.cloned.1.call-done = bf16[512,256]{1,0:T(8,128)(2,1)} async-done(((bf16[512,2048]{1,0:T(8,128)(2,1)}), bf16[512,256]{1,0:T(8,128)(2,1)}) %reduce-scatter.5.cloned.1.call-update) | async-done | bytes 262160 | tf_op jit(solution)/shard_map/reduce_scatter | solution.py:101
  419.1 1.9 pad_maximum_fusion
  (50 shorter events, 0.1 us)
Async XLA Ops:
  7.2 6.0 %copy-start.16 = (s32[4]{0:T(128)S(1)}, s32[4]{0:T(128)}, u32[]{:S(2)}) copy-start(s32[4]{0:T(128)} %param.21) | copy-start | bytes 52
  7.2 65.7 %copy-start.14 = (bf16[1,2048,352]{1,2,0:T(8,128)(2,1)S(1)}, bf16[1,2048,352]{1,2,0:T(8,128)(2,1)}, u32[]{:S(2)}) copy-start(bf16[1,2048,352]{1,2,0:T(8,128)(2,1)} %param.17) | copy-start | bytes 4325380
  7.2 65.6 %all-gather.11.cloned.1.call-start = ((), (), s32[]{:S(2)}) async-start(), calls=%async_computation.5 | async-start | bytes 2359296 | tf_op jit(solution)/shard_map/all_gather | solution.py:92
  9.2 123.7 %all-gather.9.cloned.1.call-start = ((), (), s32[]{:S(2)}) async-start(), calls=%async_computation.4 | async-start | bytes 2359296 | tf_op jit(solution)/shard_map/all_gather | solution.py:93
  11.2 254.7 %all-gather.15.cloned.1.call-start = ((), (), s32[]{:S(2)}) async-start(), calls=%async_computation.7 | async-start | bytes 2359296 | tf_op jit(solution)/shard_map/all_gather | solution.py:92
  11.9 264.7 %all-gather.13.cloned.1.call-start = ((), (), s32[]{:S(2)}) async-start(), calls=%async_computation.6 | async-start | bytes 2359296 | tf_op jit(solution)/shard_map/all_gather | solution.py:93
  12.5 327.6 %reduce-scatter.3.cloned.1.call-start = ((), (), s32[]{:S(2)}) async-start(), calls=%async_computation.2 | async-start | bytes 2359296 | tf_op jit(solution)/shard_map/reduce_scatter | solution.py:101
  13.8 61.8 %copy-start.12 = (bf16[1,2048,352]{1,2,0:T(8,128)(2,1)S(1)}, bf16[1,2048,352]{1,2,0:T(8,128)(2,1)}, u32[]{:S(2)}) copy-start(bf16[1,2048,352]{1,2,0:T(8,128)(2,1)} %param.18) | copy-start | bytes 4325380
  72.8 2.7 copy-start.19
  75.5 1.9 copy-start.21
  75.5 1.9 copy-start.11
  80.2 55.5 %copy-start.22 = (f32[512,352]{0,1:T(8,128)S(1)}, f32[512,352]{0,1:T(8,128)}, u32[]{:S(2)}) copy-start(f32[512,352]{0,1:T(8,128)} %copy-done.21) | copy-start | bytes 2162692
  80.2 338.9 %reduce-scatter.5.cloned.1.call-start = ((), (), s32[]{:S(2)}) async-start(), calls=%async_computation.3 | async-start | bytes 2359296 | tf_op jit(solution)/shard_map/reduce_scatter | solution.py:101
  133.0 2.7 copy-start.20
  135.7 3.2 copy-start.25
  169.0 2.2 copy-start.8
  169.0 2.7 copy-start.13
  171.1 3.9 copy-start.2
  171.7 2.4 copy-start.9
  171.7 2.8 copy-start.15
  172.2 96.9 %copy-start.4 = (bf16[2048,352]{0,1:T(8,128)(2,1)}, bf16[2048,352]{0,1:T(8,128)(2,1)S(1)}, u32[]{:S(2)}) copy-start(bf16[2048,352]{0,1:T(8,128)(2,1)S(1)} %fusion.14) | copy-start | bytes 4325380
  175.0 94.0 %copy-start.6 = (bf16[2048,352]{0,1:T(8,128)(2,1)}, bf16[2048,352]{0,1:T(8,128)(2,1)S(1)}, u32[]{:S(2)}) copy-start(bf16[2048,352]{0,1:T(8,128)(2,1)S(1)} %fusion.15) | copy-start | bytes 4325380
  175.0 34.6 %collective-permute-start.3 = (bf16[2048,352]{0,1:T(8,128)(2,1)S(1)}, bf16[2048,352]{0,1:T(8,128)(2,1)}, u32[]{:S(2)}, u32[]{:S(2)}) collective-permute-start(bf16[2048,352]{0,1:T(8,128)(2,1)S(1)} %get-tuple-element.87), channel_id=1, source_target_pairs={{0,16},{8,24},{16,0},{24,8},{32,48},{40,56},{48,32},{56,40},{64,80... | collective-permute-start | bytes 4325384 | tf_op jit(solution)/shard_map/cond/branch_1_fun/ppermute | solution.py:19
  175.6 65.0 %collective-permute-start.4 = (bf16[2048,352]{0,1:T(8,128)(2,1)S(1)}, bf16[2048,352]{0,1:T(8,128)(2,1)}, u32[]{:S(2)}, u32[]{:S(2)}) collective-permute-start(bf16[2048,352]{0,1:T(8,128)(2,1)S(1)} %get-tuple-element.88), channel_id=1, source_target_pairs={{0,16},{8,24},{16,0},{24,8},{32,48},{40,56},{48,32},{56,40},{64,80... | collective-permute-start | bytes 4325384 | tf_op jit(solution)/shard_map/cond/branch_1_fun/ppermute | solution.py:19
  177.2 88.7 %collective-permute-start.5 = (bf16[352,2048]{1,0:T(8,128)(2,1)S(1)}, bf16[352,2048]{1,0:T(8,128)(2,1)}, u32[]{:S(2)}, u32[]{:S(2)}) collective-permute-start(bf16[352,2048]{1,0:T(8,128)(2,1)S(1)} %get-tuple-element.89), channel_id=1, source_target_pairs={{0,16},{8,24},{16,0},{24,8},{32,48},{40,56},{48,32},{56,40},{64,80... | collective-permute-start | bytes 4325384 | tf_op jit(solution)/shard_map/cond/branch_1_fun/ppermute | solution.py:19
  265.9 3.2 copy-start.17
  269.0 3.5 copy-start.23
  269.1 3.5 copy-start.3
  276.6 3.2 copy-start.24
  276.6 3.2 copy-start.18
  279.9 3.1 copy-start.26
  315.5 2.7 copy-start.5
  315.5 2.7 copy-start.7
  315.5 3.5 copy-start.10
  318.2 5.3 %copy-start = (bf16[352,2048]{1,0:T(8,128)(2,1)}, bf16[352,2048]{1,0:T(8,128)(2,1)S(1)}, u32[]{:S(2)}) copy-start(bf16[352,2048]{1,0:T(8,128)(2,1)S(1)} %subtract_convert_fusion) | copy-start | bytes 4325380
  323.5 3.4 collective-permute-start.12
  323.6 5.4 %collective-permute-start.13 = (bf16[2048,352]{0,1:T(8,128)(2,1)S(1)}, bf16[2048,352]{0,1:T(8,128)(2,1)}, u32[]{:S(2)}, u32[]{:S(2)}) collective-permute-start(bf16[2048,352]{0,1:T(8,128)(2,1)S(1)} %get-tuple-element.97), channel_id=1, source_target_pairs={{0,8},{8,0},{16,24},{24,16},{32,40},{40,32},{48,56},{56,48},{64,72... | collective-permute-start | bytes 4325384 | tf_op jit(solution)/shard_map/cond/branch_0_fun/ppermute | solution.py:19
  324.1 7.0 %collective-permute-start.14 = (bf16[352,2048]{1,0:T(8,128)(2,1)S(1)}, bf16[352,2048]{1,0:T(8,128)(2,1)}, u32[]{:S(2)}, u32[]{:S(2)}) collective-permute-start(bf16[352,2048]{1,0:T(8,128)(2,1)S(1)} %get-tuple-element.98), channel_id=1, source_target_pairs={{0,8},{8,0},{16,24},{24,16},{32,40},{40,32},{48,56},{56,48},{64,72... | collective-permute-start | bytes 4325384 | tf_op jit(solution)/shard_map/cond/branch_0_fun/ppermute | solution.py:19
  331.0 3.1 copy-start.1
Sparse Core Ops, SparseCore 0:
  11.0 61.7 all-gather.10
  75.9 57.0 all-gather.8
  135.5 57.1 all-gather.14
  195.0 57.0 all-gather.12
  255.9 79.1 reduce-scatter.2
  339.0 80.0 reduce-scatter.4
where the time goes:
time: 428 us
  waiting for transfers between devices  287 us (67%)
  blocking collectives  43.2 us (10%)
  matrix products  43 us (10%)
  between operations  21.5 us (5%)
  other arithmetic  20.9 us (5%)
  local copies, waits for them, and re-layouts  8.34 us (2%)
    ppermute x6, waiting for transfers between devices, partner(): return lax.ppermute(value, axis, pairs)  95.1 us
    reduce_scatter x2, waiting for transfers between devices, local(): lax.psum_scatter(mixed.astype(jnp.bfloat16), 'tensor', scatter_dimension=...  79.1 us
    all_gather x2, waiting for transfers between devices, local(): lax.all_gather(inputs[step], 'tensor', axis=1, tiled=True)  59.1 us
    all_gather x2, waiting for transfers between devices, local(): lax.all_gather(out_grads[step], 'tensor', axis=1, tiled=True)  52.8 us
    psum x2, blocking collectives, total_norms(): return lax.psum((values[0],), 'tensor')  43.2 us
    convert_element_type x5, other arithmetic, apply_update(): (w.astype(jnp.float32) - scale * g).astype(jnp.bfloat16)  10 us
  transfers between devices with their start and end apart: 12, of which 9 were waited for; matrix products, arithmetic and copies ran while one was open for 15% of the time, Pallas kernels for 0%

commit v1 on v0

--- a/solution.py
+++ b/solution.py
@@ -90,7 +90,12 @@
     for step in range(inputs.shape[0]):
         whole_x, whole_dy = (
             lax.all_gather(inputs[step], "tensor", axis=1, tiled=True),
-            lax.all_gather(out_grads[step], "tensor", axis=1, tiled=True),
+            jnp.concatenate(
+                lax.all_to_all(
+                    jnp.stack([out_grads[step]] * lax.axis_size("tensor")), "tensor", 0, 0
+                ),
+                axis=1,
+            ),
         )
         bit = partner_bits[step]
         mixed, grads = local_pass(weights, whole_x, whole_dy)

time: 428 us -> 346 us (0.81)
  waiting for transfers between devices: 287 us -> 186 us
  starting transfers between devices: 3.52 us -> 14.6 us
  local copies, waits for them, and re-layouts: 8.34 us -> 13.9 us
    reduce_scatter x2, waiting for transfers between devices: 79.1 us -> 18.4 us  [local(): lax.psum_scatter(mixed.astype(jnp.bfloat16), 'tensor', scatter_dimension=...]
    all_gather x2 -> x0, waiting for transfers between devices: 52.8 us -> none  [local(): lax.all_gather(out_grads[step], 'tensor', axis=1, tiled=True)]
    all_to_all x0 -> x2, waiting for transfers between devices: none -> 30 us  [local(): lax.all_to_all(jnp.stack([out_grads[step]] * lax.axis_size('tensor')), 't...]
    all_gather x2, waiting for transfers between devices: 59.1 us -> 39.9 us  [local(): lax.all_gather(inputs[step], 'tensor', axis=1, tiled=True)]
    all_to_all x0 -> x2, starting transfers between devices: none -> 11.5 us  [local(): lax.all_to_all(jnp.stack([out_grads[step]] * lax.axis_size('tensor')), 't...]
  transfers between devices with their start and end apart: 12 -> 12, of which waited for: 9 -> 9; matrix products, arithmetic and copies ran while one was open for 15% -> 20% of each run, Pallas kernels for 0% -> 0%
where the time goes in v1:
time: 346 us; the launch traced here: 345 us
  waiting for transfers between devices  186 us (54%)
  matrix products  46.2 us (13%)
  blocking collectives  42.8 us (12%)
  between operations  21.1 us (6%)
  other arithmetic  20.7 us (6%)
  starting transfers between devices  14.6 us (4%)
  local copies, waits for them, and re-layouts  13.9 us (4%)
    ppermute x6, waiting for transfers between devices, partner(): return lax.ppermute(value, axis, pairs)  96.8 us
    psum x2, blocking collectives, total_norms(): return lax.psum((values[0],), 'tensor')  42.8 us
    all_gather x2, waiting for transfers between devices, local(): lax.all_gather(inputs[step], 'tensor', axis=1, tiled=True)  39.9 us
    all_to_all x2, waiting for transfers between devices, local(): lax.all_to_all(jnp.stack([out_grads[step]] * lax.axis_size('tensor')), 't...  30 us
    reduce_scatter x2, waiting for transfers between devices, local(): lax.psum_scatter(mixed.astype(jnp.bfloat16), 'tensor', scatter_dimension=...  18.4 us
    all_to_all x2, starting transfers between devices, local(): lax.all_to_all(jnp.stack([out_grads[step]] * lax.axis_size('tensor')), 't...  11.5 us
    convert_element_type x5, other arithmetic, apply_update(): (w.astype(jnp.float32) - scale * g).astype(jnp.bfloat16)  9.88 us
    dot_general x2, matrix products, local_pass(): lax.dot_general(inputs, d_gate, (((0,), (0,)), ((), ())), preferred_eleme...  8.17 us
  transfers between devices with their start and end apart: 12, of which 9 were waited for; matrix products, arithmetic and copies ran while one was open for 20% of the time, Pallas kernels for 0%

profile of v1, /device:TPU:32, one launch (start us, length us, event | category | flops | bytes accessed | tf_op | source)
XLA Modules:
  0.0 345.2 jit_solution(14126330136518760450)
XLA Ops:
  7.2 0.0 all-gather.5.cloned.1.call-start
  7.2 1.9 fusion.62
  9.1 0.0 all-gather.7.cloned.1.call-start
  9.1 0.7 all-gather.7.cloned.1.call-update
  9.8 1.1 slice_bitcast_fusion
  10.9 0.1 copy.53
  11.1 1.5 stack.15
  12.6 7.1 %all-to-all-start = ((bf16[8,512,256]{1,2,0:T(8,128)(2,1)}), bf16[8,512,256]{1,2,0:T(8,128)(2,1)S(1)}, u32[]{:S(2)}, u32[]{:S(2)}) async-start(bf16[8,512,256]{1,2,0:T(8,128)(2,1)} %stack.15), calls=%async_computation | async-start | bytes 4194304 | tf_op jit(solution)/shard_map/all_to_all | solution.py:94
  20.3 0.1 copy.54
  20.5 0.6 fusion.63
  21.1 30.0 %all-to-all-done = bf16[8,512,256]{1,2,0:T(8,128)(2,1)S(1)} async-done(((bf16[8,512,256]{1,2,0:T(8,128)(2,1)}), bf16[8,512,256]{1,2,0:T(8,128)(2,1)S(1)}, u32[]{:S(2)}, u32[]{:S(2)}) %all-to-all-start) | async-done | bytes 2097184 | tf_op jit(solution)/shard_map/all_to_all | solution.py:94
  51.0 1.6 stack.16
  52.6 4.5 %all-to-all-start.1 = ((bf16[8,512,256]{1,2,0:T(8,128)(2,1)}), bf16[8,512,256]{1,2,0:T(8,128)(2,1)}, u32[]{:S(2)}, u32[]{:S(2)}) async-start(bf16[8,512,256]{1,2,0:T(8,128)(2,1)} %stack.16), calls=%async_computation.1 | async-start | bytes 4194304 | tf_op jit(solution)/shard_map/all_to_all | solution.py:94
  57.1 0.0 reduce-scatter.3.cloned.1.call-start
  57.2 1.8 fusion.37
  59.0 39.9 %all-gather.5.cloned.1.call-done = bf16[1,512,2048]{2,1,0:T(8,128)(2,1)} async-done(((bf16[1,512,256]{2,1,0:T(8,128)(2,1)}), bf16[1,512,2048]{2,1,0:T(8,128)(2,1)}) %all-gather.5.cloned.1.call-update) | async-done | bytes 2097168 | tf_op jit(solution)/shard_map/all_gather | solution.py:92
  98.9 3.1 fusion.28
  102.0 1.9 multiply_convert_fusion.3
  103.9 2.7 convolution_convert_fusion.1
  106.6 0.0 reduce-scatter.3.cloned.1.call-update
  106.6 0.0 reduce-scatter.5.cloned.1.call-start
  106.7 1.5 copy-done.22
  108.2 4.9 %multiply_reduce_fusion.5 = (f32[]{:T(128)}, f32[352,2048]{1,0:T(8,128)}) fusion(bf16[1,512,2048]{2,1,0:T(8,128)(2,1)S(1)} %copy-done.22, f32[512,352]{0,1:T(8,128)} %copy-done.23, f32[512,352]{0,1:T(8,128)} %fusion.37, f32[512,352]{0,1:T(8,128)} %get-tuple-element.201), kind=kOutput, calls=%fused_computation.35 | convolution fusion | flops 741441536 | bytes 7143428 | tf_op jit(solution)/shard_map/dot_general | solution.py:38
  113.1 3.1 multiply_reduce_fusion.4
  117.5 3.2 multiply_reduce_fusion.3
  122.0 19.7 %psum.14 = f32[]{:T(128)} all-reduce(f32[]{:T(128)S(6)} %add.59), channel_id=1, replica_groups=mesh['replica'=32,'tensor'=8] {'tensor'}, use_global_device_ids=true, to_apply=%region_3.0 | all-reduce | flops 1 | bytes 8 | tf_op jit(solution)/shard_map/psum | solution.py:68
  142.3 2.0 subtract_convert_fusion.1
  144.4 0.2 copy-done.10
  144.6 0.4 copy-done.14
  145.0 0.5 fusion.14
  145.5 1.8 copy-done.9
  147.4 0.4 copy-done.15
  147.8 0.5 fusion.15
  148.3 92.2 %conditional.8 = (bf16[2048,352]{0,1:T(8,128)(2,1)}, bf16[352,2048]{1,0:T(8,128)(2,1)}, bf16[2048,352]{0,1:T(8,128)(2,1)}) conditional(s32[]{:T(128)} %bitcast.10, (bf16[2048,352]{0,1:T(8,128)(2,1)S(1)}, bf16[2048,352]{0,1:T(8,128)(2,1)S(1)}, bf16[352,2048]{1,0:T(8,128)(2,1)S(1)}) %tuple.108, ...), branch_computations={%region_4.0_spmd, %region_5.0_spmd, %region_6.0_spmd, %region_7.0_... | conditional | bytes 17301648
  148.3 0.2 collective-permute-start.3
  148.5 1.9 collective-permute-start.4
  150.4 0.1 collective-permute-start.5
  150.5 32.4 %collective-permute-done.3 = bf16[2048,352]{0,1:T(8,128)(2,1)} collective-permute-done((bf16[2048,352]{0,1:T(8,128)(2,1)S(1)}, bf16[2048,352]{0,1:T(8,128)(2,1)}, u32[]{:S(2)}, u32[]{:S(2)}) %collective-permute-start.3) | collective-permute-done | bytes 1441824 | tf_op jit(solution)/shard_map/cond/branch_1_fun/ppermute | solution.py:19
  182.9 30.9 %collective-permute-done.4 = bf16[2048,352]{0,1:T(8,128)(2,1)} collective-permute-done((bf16[2048,352]{0,1:T(8,128)(2,1)S(1)}, bf16[2048,352]{0,1:T(8,128)(2,1)}, u32[]{:S(2)}, u32[]{:S(2)}) %collective-permute-start.4) | collective-permute-done | bytes 1441824 | tf_op jit(solution)/shard_map/cond/branch_1_fun/ppermute | solution.py:19
  213.8 26.6 %collective-permute-done.5 = bf16[352,2048]{1,0:T(8,128)(2,1)} collective-permute-done((bf16[352,2048]{1,0:T(8,128)(2,1)S(1)}, bf16[352,2048]{1,0:T(8,128)(2,1)}, u32[]{:S(2)}, u32[]{:S(2)}) %collective-permute-start.5) | collective-permute-done | bytes 1441824 | tf_op jit(solution)/shard_map/cond/branch_1_fun/ppermute | solution.py:19
  240.4 3.1 fusion.43
  243.6 3.5 %multiply_convert_fusion = (bf16[512,352]{0,1:T(8,128)(2,1)S(1)}, f32[512,352]{0,1:T(8,128)}) fusion(f32[512,352]{0,1:T(8,128)S(1)} %fusion.43, bf16[1,512,2048]{2,1,0:T(8,128)(2,1)S(1)} %copy-done.19, bf16[2048,352]{0,1:T(8,128)(2,1)} %get-tuple-element.183, bf16[2048,352]{0,1:T(8,128)(2,1)S(1)} %fusion.14), kind=kOutput, calls=%fused_computation.63 | convolution fusion | flops 742883328 | bytes 6782976 | tf_op jit(solution)/shard_map/dot_general | solution.py:25
  247.1 4.0 %convolution_convert_fusion = bf16[512,2048]{1,0:T(8,128)(2,1)} fusion(bf16[512,352]{0,1:T(8,128)(2,1)S(1)} %get-tuple-element.208, bf16[352,2048]{1,0:T(8,128)(2,1)} %get-tuple-element.182, bf16[352,2048]{1,0:T(8,128)(2,1)S(1)} %copy-done.4), kind=kOutput, calls=%fused_computation | convolution fusion | flops 742850560 | bytes 5341184 | tf_op jit(solution)/shard_map/dot_general | solution.py:29
  251.1 3.9 %convolution_bitcast_fusion = f32[512,352]{0,1:T(8,128)} fusion(bf16[512,2048]{0,1:T(8,128)(2,1)} %bitcast.14, bf16[352,2048]{1,0:T(8,128)(2,1)} %get-tuple-element.182, bf16[352,2048]{1,0:T(8,128)(2,1)S(1)} %copy-done.4), kind=kOutput, calls=%fused_computation.62 | convolution fusion | flops 741801984 | bytes 5701632 | tf_op jit(solution)/shard_map/dot_general | solution.py:30
  255.0 1.6 copy-done.20
  256.6 4.6 %multiply_reduce_fusion.1 = (f32[]{:T(128)}, f32[352,2048]{1,0:T(8,128)}) fusion(bf16[1,512,2048]{2,1,0:T(8,128)(2,1)S(1)} %copy-done.20, f32[512,352]{0,1:T(8,128)} %convolution_bitcast_fusion, f32[512,352]{0,1:T(8,128)} %copy-done.25), kind=kOutput, calls=%fused_computation.30 | convolution fusion | flops 740720640 | bytes 6422532 | tf_op jit(solution)/shard_map/dot_general | solution.py:41
  261.2 3.3 multiply_reduce_fusion.2
  265.7 3.2 multiply_reduce_fusion
  270.2 23.1 %psum.15 = f32[]{:T(128)} all-reduce(f32[]{:T(128)S(6)} %add.67), channel_id=1, replica_groups=mesh['replica'=32,'tensor'=8] {'tensor'}, use_global_device_ids=true, to_apply=%region_11.0 | all-reduce | flops 1 | bytes 8 | tf_op jit(solution)/shard_map/psum | solution.py:68
  294.0 2.7 subtract_convert_fusion
  296.7 0.9 copy-done.11
  297.6 4.2 %fusion.12 = (bf16[2048,352]{0,1:T(8,128)(2,1)S(1)}, bf16[2048,352]{0,1:T(8,128)(2,1)S(1)}) fusion(f32[352,2048]{1,0:T(8,128)S(1)} %copy-done.11, f32[]{:T(128)S(6)} %div.15, bf16[2048,352]{0,1:T(8,128)(2,1)} %get-tuple-element.183, bf16[2048,352]{0,1:T(8,128)(2,1)S(1)} %copy-done.6, f32[352,2048]{1,0:T(8,128)} %get-tuple-element.205, ...), kind=kLoop, calls=%fused_computation.21 | loop fusion | flops 12976128 | bytes 14417924 | tf_op jit(solution)/shard_map/convert_element_type | solution.py:54
  301.8 7.6 %conditional.9 = (bf16[2048,352]{0,1:T(8,128)(2,1)}, bf16[2048,352]{0,1:T(8,128)(2,1)}, bf16[352,2048]{1,0:T(8,128)(2,1)}) conditional(s32[]{:T(128)} %bitcast.21, (bf16[2048,352]{0,1:T(8,128)(2,1)S(1)}, bf16[2048,352]{0,1:T(8,128)(2,1)S(1)}, bf16[352,2048]{1,0:T(8,128)(2,1)S(1)}) %tuple.109, ...), branch_computations={%region_12.0_spmd, %region_13.0_spmd, %region_14.0_spmd, %region_1... | conditional | bytes 17301648
  301.8 0.1 collective-permute-start.12
  301.9 0.5 collective-permute-start.13
  302.4 0.1 collective-permute-start.14
  302.5 2.7 collective-permute-done.12
  305.3 2.1 collective-permute-done.13
  307.4 2.1 collective-permute-done.14
  309.4 3.1 fusion.32
  312.5 3.0 fusion.34
  315.5 3.0 fusion.33
  318.4 18.4 %reduce-scatter.5.cloned.1.call-done = bf16[512,256]{1,0:T(8,128)(2,1)} async-done(((bf16[512,2048]{1,0:T(8,128)(2,1)}), bf16[512,256]{1,0:T(8,128)(2,1)}) %reduce-scatter.5.cloned.1.call-update) | async-done | bytes 262160 | tf_op jit(solution)/shard_map/reduce_scatter | solution.py:106
  336.8 1.9 pad_maximum_fusion
  (58 shorter events, 0.2 us)
Async XLA Ops:
  7.2 91.7 %all-gather.5.cloned.1.call-start = ((), (), s32[]{:S(2)}) async-start(), calls=%async_computation.6 | async-start | bytes 2359296 | tf_op jit(solution)/shard_map/all_gather | solution.py:92
  9.1 231.3 %all-gather.7.cloned.1.call-start = ((), (), s32[]{:S(2)}) async-start(), calls=%async_computation.7 | async-start | bytes 2359296 | tf_op jit(solution)/shard_map/all_gather | solution.py:92
  12.6 7.9 %copy-start.18 = (s32[4]{0:T(128)S(1)}, s32[4]{0:T(128)}, u32[]{:S(2)}) copy-start(s32[4]{0:T(128)} %param.21) | copy-start | bytes 52
  12.6 38.4 %all-to-all-start = ((bf16[8,512,256]{1,2,0:T(8,128)(2,1)}), bf16[8,512,256]{1,2,0:T(8,128)(2,1)S(1)}, u32[]{:S(2)}, u32[]{:S(2)}) async-start(bf16[8,512,256]{1,2,0:T(8,128)(2,1)} %stack.15), calls=%async_computation | async-start | bytes 4194304 | tf_op jit(solution)/shard_map/all_to_all | solution.py:94
  51.0 6.2 %copy-start = (bf16[8,512,256]{1,2,0:T(8,128)(2,1)}, bf16[8,512,256]{1,2,0:T(8,128)(2,1)S(1)}, u32[]{:S(2)}) copy-start(bf16[8,512,256]{1,2,0:T(8,128)(2,1)S(1)} %all-to-all-done) | copy-start | bytes 6291460
  52.6 4.6 %copy-start.12 = (bf16[1,352,2048]{2,1,0:T(8,128)(2,1)S(1)}, bf16[1,352,2048]{2,1,0:T(8,128)(2,1)}, u32[]{:S(2)}) copy-start(bf16[1,352,2048]{2,1,0:T(8,128)(2,1)} %param.19) | copy-start | bytes 4325380
  52.6 198.5 %all-to-all-start.1 = ((bf16[8,512,256]{1,2,0:T(8,128)(2,1)}), bf16[8,512,256]{1,2,0:T(8,128)(2,1)}, u32[]{:S(2)}, u32[]{:S(2)}) async-start(bf16[8,512,256]{1,2,0:T(8,128)(2,1)} %stack.16), calls=%async_computation.1 | async-start | bytes 4194304 | tf_op jit(solution)/shard_map/all_to_all | solution.py:94
  57.1 261.3 %reduce-scatter.3.cloned.1.call-start = ((), (), s32[]{:S(2)}) async-start(), calls=%async_computation.4 | async-start | bytes 2359296 | tf_op jit(solution)/shard_map/reduce_scatter | solution.py:106
  59.0 43.0 %copy-start.13 = (bf16[1,2048,352]{1,2,0:T(8,128)(2,1)S(1)}, bf16[1,2048,352]{1,2,0:T(8,128)(2,1)}, u32[]{:S(2)}) copy-start(bf16[1,2048,352]{1,2,0:T(8,128)(2,1)} %param.18) | copy-start | bytes 4325380
  98.9 3.1 copy-start.21
  102.0 1.9 copy-start.23
  103.9 2.7 copy-start.16
  106.6 1.6 copy-start.22
  106.6 230.2 %reduce-scatter.5.cloned.1.call-start = ((), (), s32[]{:S(2)}) async-start(), calls=%async_computation.5 | async-start | bytes 2359296 | tf_op jit(solution)/shard_map/reduce_scatter | solution.py:106
  108.2 4.9 %copy-start.24 = (f32[512,352]{0,1:T(8,128)S(1)}, f32[512,352]{0,1:T(8,128)}, u32[]{:S(2)}) copy-start(f32[512,352]{0,1:T(8,128)} %copy-done.23) | copy-start | bytes 2162692
  108.2 4.9 %copy-start.28 = (f32[512,352]{0,1:T(8,128)S(1)}, f32[512,352]{0,1:T(8,128)}, u32[]{:S(2)}) copy-start(f32[512,352]{0,1:T(8,128)} %fusion.37) | copy-start | bytes 2162692
  113.0 4.4 %copy-start.17 = (bf16[512,352]{0,1:T(8,128)(2,1)S(1)}, bf16[512,352]{0,1:T(8,128)(2,1)}, u32[]{:S(2)}) copy-start(bf16[512,352]{0,1:T(8,128)(2,1)} %copy-done.16) | copy-start | bytes 1081348
  142.3 2.3 copy-start.10
  142.3 2.7 copy-start.14
  144.4 3.9 %copy-start.3 = (bf16[352,2048]{1,0:T(8,128)(2,1)}, bf16[352,2048]{1,0:T(8,128)(2,1)S(1)}, u32[]{:S(2)}) copy-start(bf16[352,2048]{1,0:T(8,128)(2,1)S(1)} %subtract_convert_fusion.1) | copy-start | bytes 4325380
  145.0 2.3 copy-start.9
  145.0 2.7 copy-start.15
  145.5 98.1 %copy-start.5 = (bf16[2048,352]{0,1:T(8,128)(2,1)}, bf16[2048,352]{0,1:T(8,128)(2,1)S(1)}, u32[]{:S(2)}) copy-start(bf16[2048,352]{0,1:T(8,128)(2,1)S(1)} %fusion.14) | copy-start | bytes 4325380
  148.3 95.3 %copy-start.7 = (bf16[2048,352]{0,1:T(8,128)(2,1)}, bf16[2048,352]{0,1:T(8,128)(2,1)S(1)}, u32[]{:S(2)}) copy-start(bf16[2048,352]{0,1:T(8,128)(2,1)S(1)} %fusion.15) | copy-start | bytes 4325380
  148.3 34.7 %collective-permute-start.3 = (bf16[2048,352]{0,1:T(8,128)(2,1)S(1)}, bf16[2048,352]{0,1:T(8,128)(2,1)}, u32[]{:S(2)}, u32[]{:S(2)}) collective-permute-start(bf16[2048,352]{0,1:T(8,128)(2,1)S(1)} %get-tuple-element.87), channel_id=1, source_target_pairs={{0,16},{8,24},{16,0},{24,8},{32,48},{40,56},{48,32},{56,40},{64,80... | collective-permute-start | bytes 4325384 | tf_op jit(solution)/shard_map/cond/branch_1_fun/ppermute | solution.py:19
  148.5 65.4 %collective-permute-start.4 = (bf16[2048,352]{0,1:T(8,128)(2,1)S(1)}, bf16[2048,352]{0,1:T(8,128)(2,1)}, u32[]{:S(2)}, u32[]{:S(2)}) collective-permute-start(bf16[2048,352]{0,1:T(8,128)(2,1)S(1)} %get-tuple-element.88), channel_id=1, source_target_pairs={{0,16},{8,24},{16,0},{24,8},{32,48},{40,56},{48,32},{56,40},{64,80... | collective-permute-start | bytes 4325384 | tf_op jit(solution)/shard_map/cond/branch_1_fun/ppermute | solution.py:19
  150.4 90.0 %collective-permute-start.5 = (bf16[352,2048]{1,0:T(8,128)(2,1)S(1)}, bf16[352,2048]{1,0:T(8,128)(2,1)}, u32[]{:S(2)}, u32[]{:S(2)}) collective-permute-start(bf16[352,2048]{1,0:T(8,128)(2,1)S(1)} %get-tuple-element.89), channel_id=1, source_target_pairs={{0,16},{8,24},{16,0},{24,8},{32,48},{40,56},{48,32},{56,40},{64,80... | collective-permute-start | bytes 4325384 | tf_op jit(solution)/shard_map/cond/branch_1_fun/ppermute | solution.py:19
  240.4 3.2 copy-start.19
  243.6 3.5 %copy-start.25 = (f32[512,352]{0,1:T(8,128)}, f32[512,352]{0,1:T(8,128)S(1)}, u32[]{:S(2)}) copy-start(f32[512,352]{0,1:T(8,128)S(1)} %fusion.43) | copy-start | bytes 2162692
  243.6 3.5 %copy-start.4 = (bf16[352,2048]{1,0:T(8,128)(2,1)S(1)}, bf16[352,2048]{1,0:T(8,128)(2,1)}, u32[]{:S(2)}) copy-start(bf16[352,2048]{1,0:T(8,128)(2,1)} %copy-done.3) | copy-start | bytes 4325380
  255.0 1.6 copy-start.20
  256.5 4.6 %copy-start.26 = (f32[512,352]{0,1:T(8,128)S(1)}, f32[512,352]{0,1:T(8,128)}, u32[]{:S(2)}) copy-start(f32[512,352]{0,1:T(8,128)} %copy-done.25) | copy-start | bytes 2162692
  256.6 4.6 %copy-start.27 = (f32[512,352]{0,1:T(8,128)S(1)}, f32[512,352]{0,1:T(8,128)}, u32[]{:S(2)}) copy-start(f32[512,352]{0,1:T(8,128)} %convolution_bitcast_fusion) | copy-start | bytes 2162692
  256.6 4.6 %copy-start.29 = (f32[512,352]{0,1:T(8,128)S(1)}, f32[512,352]{0,1:T(8,128)}, u32[]{:S(2)}) copy-start(f32[512,352]{0,1:T(8,128)} %get-tuple-element.209) | copy-start | bytes 2162692
  293.9 2.8 copy-start.6
  294.0 2.7 copy-start.8
  294.0 3.6 %copy-start.11 = (f32[352,2048]{1,0:T(8,128)S(1)}, f32[352,2048]{1,0:T(8,128)}, u32[]{:S(2)}) copy-start(f32[352,2048]{1,0:T(8,128)} %get-tuple-element.207) | copy-start | bytes 8650756
  296.7 5.1 %copy-start.1 = (bf16[352,2048]{1,0:T(8,128)(2,1)}, bf16[352,2048]{1,0:T(8,128)(2,1)S(1)}, u32[]{:S(2)}) copy-start(bf16[352,2048]{1,0:T(8,128)(2,1)S(1)} %subtract_convert_fusion) | copy-start | bytes 4325380
  301.8 3.4 collective-permute-start.12
  301.9 5.4 %collective-permute-start.13 = (bf16[2048,352]{0,1:T(8,128)(2,1)S(1)}, bf16[2048,352]{0,1:T(8,128)(2,1)}, u32[]{:S(2)}, u32[]{:S(2)}) collective-permute-start(bf16[2048,352]{0,1:T(8,128)(2,1)S(1)} %get-tuple-element.97), channel_id=1, source_target_pairs={{0,8},{8,0},{16,24},{24,16},{32,40},{40,32},{48,56},{56,48},{64,72... | collective-permute-start | bytes 4325384 | tf_op jit(solution)/shard_map/cond/branch_0_fun/ppermute | solution.py:19
  302.4 7.0 %collective-permute-start.14 = (bf16[352,2048]{1,0:T(8,128)(2,1)S(1)}, bf16[352,2048]{1,0:T(8,128)(2,1)}, u32[]{:S(2)}, u32[]{:S(2)}) collective-permute-start(bf16[352,2048]{1,0:T(8,128)(2,1)S(1)} %get-tuple-element.98), channel_id=1, source_target_pairs={{0,8},{8,0},{16,24},{24,16},{32,40},{40,32},{48,56},{56,48},{64,72... | collective-permute-start | bytes 4325384 | tf_op jit(solution)/shard_map/cond/branch_0_fun/ppermute | solution.py:19
  309.4 3.1 copy-start.2
Sparse Core Ops, SparseCore 0:
  11.0 87.8 all-gather.4
  101.4 57.1 all-gather.6
  162.5 79.1 reduce-scatter.2
  255.1 81.6 reduce-scatter.4
